TPU v7x, 512 devices: a whole 4x8x8 slice. The times are simulated.
512 devices in a mesh: space: 64 (over x, y, z_lo), mode: 8 (over z_hi, core).
Axes of the slice: x: 4, y: 8, z: 8 (z_hi: 4, z_lo: 2; z = z_hi * 2 + z_lo), core: 2. Of those that a mesh axis runs over, the one named last changes fastest.
Arguments:
- state: float32 [858, 65536], P(None, ('space', 'mode')), may hold values from -6 to 6
- tensor: bfloat16 [64, 286, 858], P('mode'), may hold values from -0.01171875 to 0.01171875
- table: int32 [286, 3], replicated, may hold values from 0 to 10, as said below
- thermal: float32 [3], replicated, may hold values from 0.5 to 2
- output_mode_row: int32 [64], replicated, may hold values from 0 to 857, as said below
Outputs:
- updated: float32 [858, 65536], P(None, ('space', 'mode'))
- collision: float32 [64, 65536], P('mode', 'space')
Inputs may be any that keep to these rules, and one draw needn't show every extreme that they name: `table`: each row holds the three indices of one multi-index of total degree at most 10; every such multi-index is in exactly one row. `output_mode_row`: all entries are different.
All inputs are finite; a program needn't handle non-finite values.
Results may differ from a plain program's by a relative error of at most 0.004.
Values may be sent and summed in bfloat16 or wider, within the bound.
A program may use at most 64 MiB of HBM per device.

v0:
```python
import jax
import jax.numpy as jnp
from jax import lax
from jax.sharding import PartitionSpec as P

CLASSES = 3
MODES = 286


wave_bound = 5.2
courant = 0.09
collision_update = 0.1


def extended_2(x, sides, width):
    for axis, dim in sides:
        size, length = (lax.axis_size(axis), x.shape[dim])
        up = [(i, (i + 1) % size) for i in range(size)]
        down = [(j, i) for i, j in up]
        last = lax.slice_in_dim(x, length - width, length, axis=dim)
        first = lax.slice_in_dim(x, 0, width, axis=dim)
        before = lax.ppermute(last, axis, up)
        after = lax.ppermute(first, axis, down)
        x = jnp.concatenate([before, x, after], axis=dim)
    return x


def advection_matrix(table):
    codes = table[:, 0] * 144 + table[:, 1] * 12 + table[:, 2]
    along = table[:, 0].astype(jnp.float32)
    lower = (codes[None, :] == codes[:, None] - 144).astype(jnp.float32)
    higher = (codes[None, :] == codes[:, None] + 144).astype(jnp.float32)
    return jnp.sqrt(along)[:, None] * lower + jnp.sqrt(along + 1.0)[:, None] * higher


def upwind_transport(extended, state, matrix, thermal):
    blocks = extended.reshape(CLASSES, MODES, -1)
    state_after_collision = jnp.einsum(
        "ab,cbx->cax", matrix, blocks, precision=lax.Precision.HIGHEST
    )
    speed = thermal[:, None, None]
    flux = 0.5 * speed * (
        state_after_collision[:, :, :-1] + state_after_collision[:, :, 1:]
    ) - 0.5 * wave_bound * speed * (blocks[:, :, 1:] - blocks[:, :, :-1])
    change = (flux[:, :, 1:] - flux[:, :, :-1]).reshape(CLASSES * MODES, -1)
    return state - courant * change


def shards(state, tensor, table, thermal, output_mode_row):
    per_device = tensor.shape[0]
    own_modes = lax.dynamic_slice_in_dim(
        output_mode_row, lax.axis_index("mode") * per_device, per_device
    )
    mode_selector = ((own_modes // MODES)[:, None] == jnp.arange(CLASSES)[None, :]).astype(
        jnp.float32
    )
    flat = tensor.reshape(per_device * MODES, CLASSES * MODES)
    matrix = advection_matrix(table)
    piece = lax.all_gather(state.astype(jnp.bfloat16), "mode", axis=1, tiled=True)
    width = piece.shape[1]
    product = jnp.dot(flat, piece, preferred_element_type=jnp.float32).reshape(
        per_device, MODES, width
    )
    first = jnp.einsum(
        "oc,cix->oix", mode_selector, piece.reshape(CLASSES, MODES, width).astype(jnp.float32)
    )
    collision = jnp.sum(first * product, axis=1)
    extended = extended_2(state, ((("space", "mode"), 1),), 1)
    advected_state = upwind_transport(extended, state, matrix, thermal)
    own_terms = lax.all_to_all(
        collision.astype(jnp.bfloat16), "mode", split_axis=1, concat_axis=0, tiled=True
    ).astype(collision.dtype)
    placing = (jnp.arange(CLASSES * MODES)[:, None] == output_mode_row[None, :]).astype(jnp.float32)
    collision_increment = jnp.dot(
        placing, own_terms, precision=lax.Precision.HIGHEST, preferred_element_type=jnp.float32
    )
    updated = advected_state + collision_update * collision_increment
    return (updated, collision)


def solution(mesh):
    in_specs = (P(None, ("space", "mode")), P("mode", None, None), P(), P(), P())
    out_specs = (P(None, ("space", "mode")), P("mode", "space"))
    return jax.shard_map(shards, mesh=mesh, in_specs=in_specs, out_specs=out_specs, check_vma=False)
```

profile of v0, /device:TPU:1, one launch (start us, length us, event | category | flops | bytes accessed | tf_op | source)
XLA Modules:
  0.0 87.5 jit_solution(16369945874256971813)
XLA Ops:
  7.2 0.0 all-gather.2.cloned.1.call-start
  7.2 1.7 %convert_element_type.22 = bf16[858,128]{1,0:T(8,128)(2,1)} convert(f32[858,128]{1,0:T(8,128)} %param.5) | non-fusion elementwise | flops 109824 | bytes 658944 | tf_op jit(solution)/shard_map/convert_element_type | solution.py:59
  8.9 0.0 all-gather.2.cloned.1.call-update
  9.0 1.3 %fusion.26 = (f32[858,1]{1,0:T(8,128)S(1)}, f32[858,1]{1,0:T(8,128)S(1)}) fusion(f32[858,128]{1,0:T(8,128)} %param.5), kind=kLoop, calls=%fused_computation.42 | loop fusion | bytes 13728 | tf_op jit(solution)/shard_map/slice | solution.py:20
  10.3 7.2 %collective-permute-start = (f32[858,1]{1,0:T(8,128)S(1)}, f32[858,1]{1,0:T(8,128)S(1)}, u32[]{:S(2)}, u32[]{:S(2)}) collective-permute-start(f32[858,1]{1,0:T(8,128)S(1)} %get-tuple-element.9), channel_id=1, source_target_pairs={{0,1},{1,2},{2,3},{3,4},{4,5},{5,6},{6,7},{7,8},{8,9},{9,10},{10,1... | collective-permute-start | bytes 10304 | tf_op jit(solution)/shard_map/ppermute | solution.py:22
  17.5 3.5 %collective-permute-start.1 = (f32[858,1]{1,0:T(8,128)S(1)}, f32[858,1]{1,0:T(8,128)S(1)}, u32[]{:S(2)}, u32[]{:S(2)}) collective-permute-start(f32[858,1]{1,0:T(8,128)S(1)} %get-tuple-element.10), channel_id=1, source_target_pairs={{1,0},{2,1},{3,2},{4,3},{5,4},{6,5},{7,6},{8,7},{9,8},{10,9},{11,1... | collective-permute-start | bytes 10304 | tf_op jit(solution)/shard_map/ppermute | solution.py:23
  21.0 0.7 sqrt_reduce_fusion.1
  21.7 0.8 add_reduce_fusion.1
  22.5 0.7 broadcast_multiply_fusion.1
  23.2 0.7 and_select_fusion
  23.9 2.2 %collective-permute-done = f32[858,1]{1,0:T(8,128)S(1)} collective-permute-done((f32[858,1]{1,0:T(8,128)S(1)}, f32[858,1]{1,0:T(8,128)S(1)}, u32[]{:S(2)}, u32[]{:S(2)}) %collective-permute-start) | collective-permute-done | bytes 3464 | tf_op jit(solution)/shard_map/ppermute | solution.py:22
  26.2 6.9 %collective-permute-done.1 = f32[858,1]{1,0:T(8,128)S(1)} collective-permute-done((f32[858,1]{1,0:T(8,128)S(1)}, f32[858,1]{1,0:T(8,128)S(1)}, u32[]{:S(2)}, u32[]{:S(2)}) %collective-permute-start.1) | collective-permute-done | bytes 3464 | tf_op jit(solution)/shard_map/ppermute | solution.py:23
  33.1 1.4 %pad_maximum_fusion = f32[858,130]{1,0:T(8,128)S(1)} fusion(f32[858,1]{1,0:T(8,128)S(1)} %collective-permute-done.1, f32[858,128]{1,0:T(8,128)} %param.5, f32[858,1]{1,0:T(8,128)S(1)} %collective-permute-done), kind=kLoop, calls=%fused_computation.7 | loop fusion | flops 223080 | bytes 892320 | tf_op jit(solution)/shard_map/concatenate | solution.py:24
  34.5 0.1 reshape.57
  34.6 0.3 fusion.25
  34.9 0.3 copy.22
  35.2 0.3 copy.21
  35.6 3.6 %convolution_bitcast_fusion = f32[3,286,130]{1,2,0:T(8,128)S(1)} fusion(f32[3,286,130]{2,1,0:T(8,128)S(1)} %reshape.57, f32[286]{0:T(512)S(1)} %get-tuple-element.3, f32[286]{0:T(512)S(1)} %get-tuple-element.2, s32[286]{0:T(512)S(1)} %get-tuple-element.6, s32[286]{0:T(512)S(1)} %get-tuple-element.5, s32[286]{0:T(512)S(1)} %get-tuple-element.4), kind=kOutput, calls=%fused_computation.4 | convolution fusion | flops 383214272 | bytes 898040 | tf_op jit(solution)/shard_map/ab,cbx->cax/dot_general | solution.py:38
  39.2 0.2 fusion.5
  39.4 17.5 %all-gather.2.cloned.1.call-done = bf16[858,1024]{1,0:T(8,128)(2,1)} async-done(((bf16[858,128]{1,0:T(8,128)(2,1)}), bf16[858,1024]{1,0:T(8,128)(2,1)}) %all-gather.2.cloned.1.call-update) | async-done | bytes 1757200 | tf_op jit(solution)/shard_map/all_gather | solution.py:59
  56.9 1.9 %reshape.53 = bf16[3,286,1024]{2,1,0:T(8,128)(2,1)S(1)} reshape(bf16[858,1024]{1,0:T(8,128)(2,1)} %all-gather.2.cloned.1.call-done) | data formatting | bytes 3514368 | tf_op jit(solution)/shard_map/reshape | solution.py:65
  58.8 0.0 copy-start.1
  58.8 0.0 copy-start.4
  58.8 1.8 %fusion = f32[8,286,1024]{2,0,1:T(8,128)S(1)} fusion(bf16[3,286,1024]{2,1,0:T(8,128)(2,1)S(1)} %reshape.53, s32[8]{0:T(128)S(1)} %and_select_fusion), kind=kOutput, calls=%fused_computation.1 | convolution fusion | flops 14057496 | bytes 11128864 | tf_op jit(solution)/shard_map/oc,cix->oix/dot_general | solution.py:64
  60.6 0.0 copy-done.1
  60.6 0.9 copy-done.4
  61.5 0.0 copy-start
  61.5 0.0 copy-start.3
  61.5 5.4 %multiply_reduce_fusion = f32[8,1024]{1,0:T(8,128)S(1)} fusion(f32[8,286,1024]{2,0,1:T(8,128)S(1)} %fusion, bf16[8,286,858]{2,0,1:T(8,128)(2,1)S(1)} %copy-done.4, bf16[858,1024]{1,0:T(8,128)(2,1)S(1)} %copy-done.1), kind=kOutput, calls=%fused_computation | convolution fusion | flops 4025114624 | bytes 15087808 | tf_op jit(solution)/shard_map/dot_general | solution.py:61
  66.9 0.0 copy-start.2
  66.9 0.6 convert_bitcast_fusion
  67.5 5.0 %all-to-all-start = ((bf16[8,8,128]{2,0,1:T(8,128)(2,1)}), bf16[8,8,128]{2,0,1:T(8,128)(2,1)S(1)}, u32[]{:S(2)}, u32[]{:S(2)}) async-start(bf16[8,8,128]{2,0,1:T(8,128)(2,1)} %convert_bitcast_fusion), calls=%async_computation | async-start | bytes 32768 | tf_op jit(solution)/shard_map/all_to_all | solution.py:70
  72.5 0.1 fusion.6
  72.6 0.2 copy.13
  72.9 6.7 %all-to-all-done = bf16[8,8,128]{2,0,1:T(8,128)(2,1)S(1)} async-done(((bf16[8,8,128]{2,0,1:T(8,128)(2,1)}), bf16[8,8,128]{2,0,1:T(8,128)(2,1)S(1)}, u32[]{:S(2)}, u32[]{:S(2)}) %all-to-all-start) | async-done | bytes 16416 | tf_op jit(solution)/shard_map/all_to_all | solution.py:70
  79.6 0.0 copy-done
  79.6 0.0 copy-done.3
  79.6 1.0 %fusion.3 = f32[858,128]{1,0:T(8,128)} fusion(f32[858,128]{1,0:T(8,128)S(1)} %copy-done, f32[858,128]{1,0:T(8,128)S(1)} %mul.109, s32[64]{0:T(128)S(1)} %copy-done.3, bf16[8,8,128]{2,0,1:T(8,128)(2,1)S(1)} %all-to-all-done), kind=kOutput, calls=%fused_computation.6 | convolution fusion | flops 14441856 | bytes 1334528 | tf_op jit(solution)/shard_map/dot_general | solution.py:74
  80.6 0.0 copy-done.2
  (1 shorter events, 0.0 us)
Async XLA Ops:
  7.2 49.7 %all-gather.2.cloned.1.call-start = ((), (), s32[]{:S(2)}) async-start(), calls=%async_computation.1 | async-start | bytes 1990656 | tf_op jit(solution)/shard_map/all_gather | solution.py:59
  10.3 15.9 %collective-permute-start = (f32[858,1]{1,0:T(8,128)S(1)}, f32[858,1]{1,0:T(8,128)S(1)}, u32[]{:S(2)}, u32[]{:S(2)}) collective-permute-start(f32[858,1]{1,0:T(8,128)S(1)} %get-tuple-element.9), channel_id=1, source_target_pairs={{0,1},{1,2},{2,3},{3,4},{4,5},{5,6},{6,7},{7,8},{8,9},{9,10},{10,1... | collective-permute-start | bytes 10304 | tf_op jit(solution)/shard_map/ppermute | solution.py:22
  17.5 15.6 %collective-permute-start.1 = (f32[858,1]{1,0:T(8,128)S(1)}, f32[858,1]{1,0:T(8,128)S(1)}, u32[]{:S(2)}, u32[]{:S(2)}) collective-permute-start(f32[858,1]{1,0:T(8,128)S(1)} %get-tuple-element.10), channel_id=1, source_target_pairs={{1,0},{2,1},{3,2},{4,3},{5,4},{6,5},{7,6},{8,7},{9,8},{10,9},{11,1... | collective-permute-start | bytes 10304 | tf_op jit(solution)/shard_map/ppermute | solution.py:23
  58.8 1.8 %copy-start.1 = (bf16[858,1024]{1,0:T(8,128)(2,1)S(1)}, bf16[858,1024]{1,0:T(8,128)(2,1)}, u32[]{:S(2)}) copy-start(bf16[858,1024]{1,0:T(8,128)(2,1)} %all-gather.2.cloned.1.call-done) | copy-start | bytes 5271556
  58.8 2.7 %copy-start.4 = (bf16[8,286,858]{2,0,1:T(8,128)(2,1)S(1)}, bf16[8,286,858]{2,0,1:T(8,128)(2,1)}, u32[]{:S(2)}) copy-start(bf16[8,286,858]{2,0,1:T(8,128)(2,1)} %param.6) | copy-start | bytes 11778628
  61.5 18.1 %copy-start = (f32[858,128]{1,0:T(8,128)S(1)}, f32[858,128]{1,0:T(8,128)}, u32[]{:S(2)}) copy-start(f32[858,128]{1,0:T(8,128)} %param.5) | copy-start | bytes 1317892
  61.5 18.1 %copy-start.3 = (s32[64]{0:T(128)S(1)}, s32[64]{0:T(128)}, u32[]{:S(2)}) copy-start(s32[64]{0:T(128)} %param.9) | copy-start | bytes 772
  66.9 13.7 %copy-start.2 = (f32[8,1024]{1,0:T(8,128)}, f32[8,1024]{1,0:T(8,128)S(1)}, u32[]{:S(2)}) copy-start(f32[8,1024]{1,0:T(8,128)S(1)} %multiply_reduce_fusion) | copy-start | bytes 98308
  67.5 12.1 %all-to-all-start = ((bf16[8,8,128]{2,0,1:T(8,128)(2,1)}), bf16[8,8,128]{2,0,1:T(8,128)(2,1)S(1)}, u32[]{:S(2)}, u32[]{:S(2)}) async-start(bf16[8,8,128]{2,0,1:T(8,128)(2,1)} %convert_bitcast_fusion), calls=%async_computation | async-start | bytes 32768 | tf_op jit(solution)/shard_map/all_to_all | solution.py:70
Sparse Core Ops, SparseCore 0:
  10.7 46.1 all-gather.1
where the time goes:
time: 88.5 us; the launch traced here: 87.5 us
  waiting for transfers between devices  33.4 us (38%)
  starting transfers between devices  15.7 us (18%)
  between operations  14.2 us (16%)
  matrix products  11.8 us (13%)
  other arithmetic  7 us (8%)
  local copies, waits for them, and re-layouts  5.42 us (6%)
    all_gather x1, waiting for transfers between devices, shards(): lax.all_gather(state.astype(jnp.bfloat16), 'mode', axis=1, tiled=True)  17.5 us
    ppermute x1, starting transfers between devices, extended_2(): before = lax.ppermute(last, axis, up)  7.19 us
    ppermute x1, waiting for transfers between devices, extended_2(): after = lax.ppermute(first, axis, down)  6.92 us
    all_to_all x1, waiting for transfers between devices, shards(): lax.all_to_all(collision.astype(jnp.bfloat16), 'mode', split_axis=1, conc...  6.74 us
    dot_general x1, matrix products, shards(): jnp.dot(flat, piece, preferred_element_type=jnp.float32)  5.42 us
    all_to_all x1, starting transfers between devices, shards(): lax.all_to_all(collision.astype(jnp.bfloat16), 'mode', split_axis=1, conc...  5 us
    dot_general x1, matrix products, upwind_transport(): jnp.einsum('ab,cbx->cax', matrix, blocks, precision=lax.Precision.HIGHEST)  3.58 us
    ppermute x1, starting transfers between devices, extended_2(): after = lax.ppermute(first, axis, down)  3.48 us
  transfers between devices with their start and end apart: 4, of which 4 were waited for; matrix products, arithmetic and copies ran while one was open for 12% of the time, Pallas kernels for 0%

commit v1 on v0

v1 whole, which is shorter than its diff:
```python
import functools

import jax
import jax.numpy as jnp
from jax import lax
from jax.experimental import pallas as pl
from jax.experimental.pallas import tpu as pltpu
from jax.sharding import PartitionSpec as P

CLASSES = 3
MODES = 286
ROWS = CLASSES * MODES
PAD = 864
HALF = 432
OWN = 8
TILE_I = 26
TILES_I = MODES // TILE_I

wave_bound = 5.2
courant = 0.09
collision_update = 0.1

MESH = pl.DeviceIdType.MESH


def kernel(
    spaces,
    state_hbm,
    tensor_hbm,
    table_hbm,
    thermal_hbm,
    target_hbm,
    updated_ref,
    collision_ref,
    state,
    tensor,
    table,
    thermal,
    target,
    slab,
    first,
    terms_out,
    terms,
    edge_out,
    edge_in,
    matrix,
    delta,
    base,
    placing,
    load_sem,
    z_send,
    z_recv,
    c_send,
    c_recv,
    t_send,
    t_recv,
    e_send,
    e_recv,
):
    space = lax.axis_index("space")
    me = lax.axis_index("mode")
    q, c = me // 2, me % 2
    partner = me + 1 - 2 * c
    right_q, left_q, far_q = (q + 1) % 4, (q + 3) % 4, (q + 2) % 4
    right, left, far = 2 * right_q + c, 2 * left_q + c, 2 * far_q + c

    after = me + 1
    before = me + 7
    after_space = (space + after // 8) % spaces
    before_space = (space + spaces - 1 + before // 8) % spaces
    after_id = {"space": after_space, "mode": after % 8}
    before_id = {"space": before_space, "mode": before % 8}

    barrier = pltpu.get_barrier_semaphore()
    for step in range(1, 8):
        pl.semaphore_signal(
            barrier, inc=1, device_id={"mode": (me + step) % 8}, device_id_type=MESH
        )
    pl.semaphore_signal(barrier, inc=1, device_id=after_id, device_id_type=MESH)
    pl.semaphore_signal(barrier, inc=1, device_id=before_id, device_id_type=MESH)

    def load(source, dest, sem):
        copy = pltpu.make_async_copy(source, dest, load_sem.at[sem])
        copy.start()
        return copy

    state_load = load(state_hbm, state.at[pl.ds(0, ROWS)], 0)
    tensor_load = load(tensor_hbm, tensor, 1)
    table_load = load(table_hbm, table, 2)
    thermal_load = load(thermal_hbm, thermal, 3)
    target_load = load(target_hbm, target, 4)

    def remote(source, dest, send, recv, device):
        return pltpu.make_async_remote_copy(
            src_ref=source,
            dst_ref=dest,
            send_sem=send,
            recv_sem=recv,
            device_id=device,
            device_id_type=MESH,
        )

    def half(slot, h):
        return slab.at[slot, pl.ds(h * HALF, HALF)]

    def over_z(slot, h, i, device):
        return remote(half(slot, h), half(slot, h), z_send.at[i], z_recv.at[i], {"mode": device})

    def over_chip(slot, h, i):
        return remote(half(slot, h), half(slot, h), c_send.at[i], c_recv.at[i], {"mode": partner})

    state_load.wait()
    state[pl.ds(ROWS, 896 - ROWS), :] = jnp.zeros((896 - ROWS, 128), jnp.float32)
    slab[me] = state[pl.ds(0, PAD), :].astype(jnp.bfloat16)
    pl.semaphore_wait(barrier, 9)

    sends = [
        over_z(me, 0, 0, right),
        over_z(me, 1, 3, left),
        over_z(me, 1, 1, right),
        over_z(me, 0, 4, left),
        over_chip(me, 0, 0),
        over_chip(me, 1, 1),
    ]
    for copy in sends:
        copy.start()

    edge_out[...] = jnp.zeros_like(edge_out)
    for t in range(7):
        turned = jnp.transpose(state[pl.ds(128 * t, 128), :])
        edge_out[0, pl.ds(t, 1), :] = turned[0:1, :]
        edge_out[1, pl.ds(t, 1), :] = turned[127:128, :]
    edges = [
        remote(edge_out.at[0], edge_in.at[1], e_send.at[0], e_recv.at[0], before_id),
        remote(edge_out.at[1], edge_in.at[0], e_send.at[1], e_recv.at[1], after_id),
    ]
    for copy in edges:
        copy.start()

    table_load.wait()
    thermal_load.wait()
    target_load.wait()
    along = table[0:1, :]
    codes = along * 144 + table[1:2, :] * 12 + table[2:3, :]
    spread = jnp.broadcast_to(
        jnp.concatenate([codes.astype(jnp.float32), jnp.zeros((1, 384 - MODES), jnp.float32)], axis=1),
        (128, 384),
    )
    code_column = jnp.transpose(spread)[:MODES, 0:1]
    n = along.astype(jnp.float32)
    gap = code_column - codes.astype(jnp.float32)
    matrix[...] = jnp.where(gap == 144.0, jnp.sqrt(n + 1.0), 0.0) + jnp.where(
        gap == -144.0, jnp.sqrt(n), 0.0
    )
    row_index = lax.broadcasted_iota(jnp.int32, (ROWS, 64), 0)
    placing[...] = jnp.where(row_index == target[...], 1.0, 0.0).astype(jnp.bfloat16)

    spot = lax.broadcasted_iota(jnp.int32, (OWN, 64), 1) - lax.broadcasted_iota(
        jnp.int32, (OWN, 64), 0
    )
    own_target = jnp.sum(
        jnp.where(spot == me * OWN, target[...].astype(jnp.float32), 0.0), axis=1, keepdims=True
    )
    wide = jnp.broadcast_to(own_target, (OWN, 256))
    in_first = wide < float(MODES)
    in_second = wide < float(2 * MODES)

    def collide(chip):
        rhs = jnp.concatenate([slab[2 * chip], slab[2 * chip + 1]], axis=1)[:ROWS, :]
        first[...] = rhs.astype(jnp.float32)

        def tile(k, acc):
            lhs = tensor[pl.ds(pl.multiple_of(k * (TILE_I * OWN), 8), TILE_I * OWN), :]
            product = jnp.dot(lhs, rhs, preferred_element_type=jnp.float32)
            for j in range(TILE_I):
                i = k * TILE_I + j
                rows = [
                    jnp.broadcast_to(first[pl.ds(i + MODES * d, 1), :], (OWN, 256))
                    for d in range(CLASSES)
                ]
                chosen = jnp.where(in_first, rows[0], jnp.where(in_second, rows[1], rows[2]))
                acc = acc + chosen * product[OWN * j : OWN * (j + 1), :]
            return acc

        total = lax.fori_loop(0, TILES_I, tile, jnp.zeros((OWN, 256), jnp.float32))
        terms_out[2 * chip] = total[:, :128]
        terms_out[2 * chip + 1] = total[:, 128:]

    def give(slot):
        return remote(
            terms_out.at[slot], terms.at[me], t_send.at[slot], t_recv.at[me], {"mode": slot}
        )

    tensor_load.wait()
    over_chip(partner, 0, 0).wait_recv()
    over_chip(partner, 1, 1).wait_recv()
    collide(q)
    terms[me] = terms_out[me]
    give(partner).start()

    over_z(left, 0, 0, right).wait_recv()
    passed = [over_z(left, 0, 2, right), over_chip(left, 0, 2)]
    for copy in passed:
        copy.start()
    over_z(right, 1, 3, left).wait_recv()
    more = [over_z(right, 1, 5, left), over_chip(right, 1, 3)]
    for copy in more:
        copy.start()
    passed += more

    edges[0].wait_recv()
    edges[1].wait_recv()
    turned = jnp.transpose(
        jnp.concatenate(
            [edge_in[0], edge_in[1], jnp.zeros((112, 128), jnp.float32)], axis=0
        )
    )
    lane = lax.broadcasted_iota(jnp.int32, (128, 128), 1)
    speed = [thermal[0:1, d : d + 1] for d in range(CLASSES)]
    for t in range(7):
        x = state[pl.ds(128 * t, 128), :]
        lower = jnp.where(lane == 0, turned[:, t : t + 1], pltpu.roll(x, 1, 1))
        upper = jnp.where(lane == 127, turned[:, 8 + t : 9 + t], pltpu.roll(x, 127, 1))
        row = lax.broadcasted_iota(jnp.int32, (128, 128), 0) + 128 * t
        scale = jnp.where(row < MODES, speed[0], jnp.where(row < 2 * MODES, speed[1], speed[2]))
        delta[pl.ds(128 * t, 128), :] = (0.5 * courant) * scale * (upper - lower)
        base[pl.ds(128 * t, 128), :] = x + (0.5 * courant * wave_bound) * scale * (
            (upper - x) - (x - lower)
        )
    for d in range(CLASSES):
        rows = pl.ds(MODES * d, MODES)
        base[rows, :] = base[rows, :] - jnp.dot(
            matrix[...],
            delta[rows, :],
            precision=lax.Precision.HIGHEST,
            preferred_element_type=jnp.float32,
        )

    over_z(left, 1, 1, right).wait_recv()
    over_z(right, 0, 4, left).wait_recv()
    more = [over_chip(left, 1, 4), over_chip(right, 0, 5)]
    for copy in more:
        copy.start()
    passed += more
    left_other, right_other, far_other = (2 * v + 1 - c for v in (left_q, right_q, far_q))
    over_chip(left_other, 0, 2).wait_recv()
    over_chip(left_other, 1, 4).wait_recv()
    collide(left_q)
    give(left).start()
    give(left_other).start()
    over_chip(right_other, 1, 3).wait_recv()
    over_chip(right_other, 0, 5).wait_recv()
    collide(right_q)
    give(right).start()
    give(right_other).start()

    over_z(far, 0, 2, right).wait_recv()
    over_z(far, 1, 5, left).wait_recv()
    more = [over_chip(far, 0, 6), over_chip(far, 1, 7)]
    for copy in more:
        copy.start()
    passed += more
    over_chip(far_other, 0, 6).wait_recv()
    over_chip(far_other, 1, 7).wait_recv()
    collide(far_q)
    give(far).start()
    give(far_other).start()
    for slot in range(8):
        collision_ref[:, 128 * slot : 128 * (slot + 1)] = terms_out[slot]

    others = (partner, left, left_other, right, right_other, far, far_other)
    for other in others:
        remote(
            terms_out.at[other], terms.at[other], t_send.at[other], t_recv.at[other], {"mode": other}
        ).wait_recv()
    scaled = collision_update * terms[...].reshape(64, 128)
    high = scaled.astype(jnp.bfloat16)
    low = (scaled - high.astype(jnp.float32)).astype(jnp.bfloat16)
    updated_ref[...] = (
        base[pl.ds(0, ROWS), :]
        + jnp.dot(placing[...], high, preferred_element_type=jnp.float32)
        + jnp.dot(placing[...], low, preferred_element_type=jnp.float32)
    )
    for copy in sends + passed + edges:
        copy.wait_send()
    for other in others:
        give(other).wait_send()


def shards(spaces, state, tensor, table, thermal, output_mode_row):
    f32, bf16 = jnp.float32, jnp.bfloat16
    flat = jnp.transpose(tensor, (1, 0, 2)).reshape(MODES * OWN, ROWS)
    anywhere = pl.BlockSpec(memory_space=pl.ANY)
    return pl.pallas_call(
        functools.partial(kernel, spaces),
        out_shape=(
            jax.ShapeDtypeStruct((ROWS, 128), f32),
            jax.ShapeDtypeStruct((OWN, 1024), f32),
        ),
        in_specs=[anywhere] * 5,
        out_specs=(pl.BlockSpec(memory_space=pltpu.VMEM),) * 2,
        scratch_shapes=[
            pltpu.VMEM((896, 128), f32),
            pltpu.VMEM((MODES * OWN, ROWS), bf16),
            pltpu.VMEM((3, MODES), jnp.int32),
            pltpu.VMEM((1, CLASSES), f32),
            pltpu.VMEM((1, 64), jnp.int32),
            pltpu.VMEM((8, PAD, 128), bf16),
            pltpu.VMEM((ROWS, 256), f32),
            pltpu.VMEM((8, OWN, 128), f32),
            pltpu.VMEM((8, OWN, 128), f32),
            pltpu.VMEM((2, 8, 128), f32),
            pltpu.VMEM((2, 8, 128), f32),
            pltpu.VMEM((MODES, MODES), f32),
            pltpu.VMEM((896, 128), f32),
            pltpu.VMEM((896, 128), f32),
            pltpu.VMEM((ROWS, 64), bf16),
            pltpu.SemaphoreType.DMA((5,)),
            pltpu.SemaphoreType.DMA((6,)),
            pltpu.SemaphoreType.DMA((6,)),
            pltpu.SemaphoreType.DMA((8,)),
            pltpu.SemaphoreType.DMA((8,)),
            pltpu.SemaphoreType.DMA((8,)),
            pltpu.SemaphoreType.DMA((8,)),
            pltpu.SemaphoreType.DMA((2,)),
            pltpu.SemaphoreType.DMA((2,)),
        ],
        compiler_params=pltpu.CompilerParams(collective_id=0, has_side_effects=True),
    )(state, flat, table.T, thermal.reshape(1, CLASSES), output_mode_row.reshape(1, 64))


def solution(mesh):
    in_specs = (P(None, ("space", "mode")), P("mode", None, None), P(), P(), P())
    out_specs = (P(None, ("space", "mode")), P("mode", "space"))
    return jax.shard_map(
        functools.partial(shards, mesh.shape["space"]),
        mesh=mesh,
        in_specs=in_specs,
        out_specs=out_specs,
        check_vma=False,
    )
```

time: 88.5 us -> 48.9 us (0.55)
  the two profiles are of different devices: /device:TPU:1 before, /device:TPU:125 now
where the time goes in v1:
time: 48.9 us; the launch traced here: 48.7 us
  Pallas kernels  44.9 us (92%)
  local copies, waits for them, and re-layouts  3.18 us (7%)
  between operations  0.64 us (1%)
    pallas_call x1, Pallas kernels, shards(): pl.pallas_call(functools.partial(kernel, spaces), out_shape=(jax.ShapeDty...  44.9 us
    unnamed x2, local copies, waits for them, and re-layouts  3.18 us

profile of v1, /device:TPU:125, one launch (start us, length us, event | category | flops | bytes accessed | tf_op | source)
XLA Modules:
  0.0 48.7 jit_solution(14458737549926143981)
XLA Ops:
  0.6 44.9 %shard_map.68 = (f32[858,128]{1,0:T(8,128)}, f32[8,1024]{1,0:T(8,128)}) custom-call(f32[858,128]{1,0:T(8,128)} %state_hbm.1, bf16[2288,858]{1,0:T(8,128)(2,1)} %bitcast.6, s32[3,286]{1,0:T(4,128)} %bitcast.7, f32[1,3]{1,0:T(1,128)} %bitcast.8, s32[1,64]{1,0:T(1,128)} %bitcast.9), custom_call_target="tpu_custom_call" | custom-call | tf_op jit(solution)/shard_map/pallas_call | solution.py:294
  45.5 1.8 %copy.9 = f32[858,128]{1,0:T(8,128)} copy(f32[858,128]{1,0:T(8,128)} %get-tuple-element.4) | data formatting | bytes 878592
  47.3 1.4 %copy.10 = f32[8,1024]{1,0:T(8,128)} copy(f32[8,1024]{1,0:T(8,128)} %get-tuple-element.5) | data formatting | bytes 65536

commit v2 on v1

v2 whole, which is shorter than its diff:
```python
import functools

import jax
import jax.numpy as jnp
from jax import lax
from jax.experimental import pallas as pl
from jax.experimental.pallas import tpu as pltpu
from jax.sharding import PartitionSpec as P

CLASSES = 3
MODES = 286
ROWS = CLASSES * MODES
PAD = 864
HALF = 432
OWN = 8

wave_bound = 5.2
courant = 0.09
collision_update = 0.1

MESH = pl.DeviceIdType.MESH


def kernel(
    spaces,
    state_hbm,
    tensor_hbm,
    table_hbm,
    thermal_hbm,
    target_hbm,
    updated,
    terms_out,
    state,
    tensor,
    table,
    thermal,
    target,
    slab,
    first,
    terms,
    edge_out,
    edge_in,
    matrix,
    delta,
    base,
    placing,
    load_sem,
    z_send,
    z_recv,
    c_send,
    c_recv,
    t_send,
    t_recv,
    e_send,
    e_recv,
):
    space = lax.axis_index("space")
    me = lax.axis_index("mode")
    q, c = me // 2, me % 2
    partner = me + 1 - 2 * c
    right_q, left_q, far_q = (q + 1) % 4, (q + 3) % 4, (q + 2) % 4
    right, left, far = 2 * right_q + c, 2 * left_q + c, 2 * far_q + c

    after = me + 1
    before = me + 7
    after_space = (space + after // 8) % spaces
    before_space = (space + spaces - 1 + before // 8) % spaces
    after_id = {"space": after_space, "mode": after % 8}
    before_id = {"space": before_space, "mode": before % 8}

    sideways_id = {
        "space": jnp.where(c == 0, before_id["space"], after_id["space"]),
        "mode": jnp.where(c == 0, before_id["mode"], after_id["mode"]),
    }

    barrier = pltpu.get_barrier_semaphore()
    for device in ({"mode": right}, {"mode": left}, {"mode": partner}, sideways_id):
        pl.semaphore_signal(barrier, inc=1, device_id=device, device_id_type=MESH)

    def load(source, dest, sem):
        copy = pltpu.make_async_copy(source, dest, load_sem.at[sem])
        copy.start()
        return copy

    state_load = load(state_hbm, state.at[pl.ds(0, ROWS)], 0)
    table_load = load(table_hbm, table, 2)
    thermal_load = load(thermal_hbm, thermal, 3)
    target_load = load(target_hbm, target, 4)

    def remote(source, dest, send, recv, device):
        return pltpu.make_async_remote_copy(
            src_ref=source,
            dst_ref=dest,
            send_sem=send,
            recv_sem=recv,
            device_id=device,
            device_id_type=MESH,
        )

    def half(slot, h):
        return slab.at[slot, pl.ds(pl.multiple_of(h * HALF, 16), HALF)]

    def over_z(slot, h, i, device):
        return remote(half(slot, h), half(slot, h), z_send.at[i], z_recv.at[i], {"mode": device})

    def over_chip(slot, h, i):
        return remote(half(slot, h), half(slot, h), c_send.at[i], c_recv.at[i], {"mode": partner})

    state_load.wait()
    tensor_load = load(tensor_hbm, tensor, 1)
    state[pl.ds(ROWS, 896 - ROWS), :] = jnp.zeros((896 - ROWS, 128), jnp.float32)
    slab[me] = state[pl.ds(0, PAD), :].astype(jnp.bfloat16)

    edge_out[...] = jnp.zeros_like(edge_out)
    for t in range(7):
        turned = jnp.transpose(state[pl.ds(128 * t, 128), :])
        edge_out[0, pl.ds(t, 1), :] = turned[0:1, :]
        edge_out[1, pl.ds(t, 1), :] = turned[127:128, :]
    edges = [
        remote(edge_out.at[0], edge_in.at[1], e_send.at[0], e_recv.at[0], before_id),
        remote(edge_out.at[1], edge_in.at[0], e_send.at[1], e_recv.at[1], after_id),
    ]
    pl.semaphore_wait(barrier, 4)

    own = [
        over_z(me, 0, 0, right),
        over_z(me, 1, 1, left),
        over_z(me, 1, 2, right),
        over_z(me, 0, 3, left),
        over_chip(me, 0, 0),
        over_chip(me, 1, 1),
    ]
    for copy in edges + own:
        copy.start()

    table_load.wait()
    thermal_load.wait()
    target_load.wait()
    along = table[0:1, :]
    codes = along * 144 + table[1:2, :] * 12 + table[2:3, :]
    spread = jnp.broadcast_to(
        jnp.concatenate([codes.astype(jnp.float32), jnp.zeros((1, 384 - MODES), jnp.float32)], axis=1),
        (128, 384),
    )
    code_column = jnp.transpose(spread)[:MODES, 0:1]
    n = along.astype(jnp.float32)
    gap = code_column - codes.astype(jnp.float32)
    matrix[...] = jnp.where(gap == 144.0, jnp.sqrt(n + 1.0), 0.0) + jnp.where(
        gap == -144.0, jnp.sqrt(n), 0.0
    )
    row_index = lax.broadcasted_iota(jnp.int32, (ROWS, 64), 0)
    placing[...] = jnp.where(row_index == target[...], 1.0, 0.0).astype(jnp.bfloat16)

    spot = lax.broadcasted_iota(jnp.int32, (OWN, 64), 1) - lax.broadcasted_iota(
        jnp.int32, (OWN, 64), 0
    )
    own_target = jnp.sum(
        jnp.where(spot == me * OWN, target[...].astype(jnp.float32), 0.0), axis=1, keepdims=True
    )
    wide = jnp.broadcast_to(own_target, (OWN, 256))
    in_first = wide < float(MODES)
    in_second = wide < float(2 * MODES)

    def transport():
        edges[0].wait_recv()
        edges[1].wait_recv()
        turned = jnp.transpose(
            jnp.concatenate(
                [edge_in[0], edge_in[1], jnp.zeros((112, 128), jnp.float32)], axis=0
            )
        )
        lane = lax.broadcasted_iota(jnp.int32, (128, 128), 1)
        speed = [thermal[0:1, d : d + 1] for d in range(CLASSES)]
        for t in range(7):
            x = state[pl.ds(128 * t, 128), :]
            lower = jnp.where(lane == 0, turned[:, t : t + 1], pltpu.roll(x, 1, 1))
            upper = jnp.where(lane == 127, turned[:, 8 + t : 9 + t], pltpu.roll(x, 127, 1))
            row = lax.broadcasted_iota(jnp.int32, (128, 128), 0) + 128 * t
            scale = jnp.where(
                row < MODES, speed[0], jnp.where(row < 2 * MODES, speed[1], speed[2])
            )
            delta[pl.ds(128 * t, 128), :] = (0.5 * courant) * scale * (upper - lower)
            base[pl.ds(128 * t, 128), :] = x + (0.5 * courant * wave_bound) * scale * (
                (upper - x) - (x - lower)
            )
        for d in range(CLASSES):
            rows = pl.ds(MODES * d, MODES)
            base[rows, :] = base[rows, :] - jnp.dot(
                matrix[...],
                delta[rows, :],
                precision=lax.Precision.HIGHEST,
                preferred_element_type=jnp.float32,
            )

    def give(slot):
        return remote(
            terms_out.at[slot], terms.at[me], t_send.at[slot], t_recv.at[me], {"mode": slot}
        )

    def take(other):
        return remote(
            terms_out.at[other], terms.at[other], t_send.at[other], t_recv.at[other], {"mode": other}
        )

    near = jnp.where((q == 0) | (q == 3), 1, 0)
    sides = (near, 1 - near)

    def side_chip(side):
        return jnp.where(side == 0, left_q, right_q)

    def pass_early(side):
        slot, back = 2 * side_chip(side) + c, 2 * side_chip(1 - side) + c
        over_z(slot, side, side, back).wait_recv()
        over_z(slot, side, 4 + side, back).start()
        over_chip(slot, side, 2 + side).start()

    def pass_late(side):
        slot, back = 2 * side_chip(side) + c, 2 * side_chip(1 - side) + c
        over_z(slot, 1 - side, 2 + side, back).wait_recv()
        over_chip(slot, 1 - side, 4 + side).start()

    def await_partner(side):
        slot = 2 * side_chip(side) + 1 - c
        over_chip(slot, side, 2 + side).wait_recv()
        over_chip(slot, 1 - side, 4 + side).wait_recv()

    def step(k, carry):
        @pl.when(k == 0)
        def _():
            tensor_load.wait()
            over_chip(partner, 0, 0).wait_recv()
            over_chip(partner, 1, 1).wait_recv()

        @pl.when(k == 1)
        def _():
            pass_early(0)
            pass_early(1)
            transport()
            pass_late(sides[0])
            pass_late(sides[1])
            await_partner(sides[0])

        @pl.when(k == 2)
        def _():
            await_partner(sides[1])

        @pl.when(k == 3)
        def _():
            for side in range(2):
                over_z(far, side, 4 + side, right).wait_recv()
                over_chip(far, side, 6 + side).start()
            for side in range(2):
                over_chip(2 * far_q + 1 - c, side, 6 + side).wait_recv()

        chip = jnp.where(
            k == 0, q, jnp.where(k == 1, side_chip(near), jnp.where(k == 2, side_chip(1 - near), far_q))
        )
        rhs = jnp.concatenate([slab[2 * chip], slab[2 * chip + 1]], axis=1)[:ROWS, :]
        first[...] = rhs.astype(jnp.float32)
        product = jnp.dot(tensor[...], rhs, preferred_element_type=jnp.float32)
        total = [jnp.zeros((OWN, 256), jnp.float32)] * 4
        for i in range(MODES):
            rows = [
                jnp.broadcast_to(first[pl.ds(i + MODES * d, 1), :], (OWN, 256))
                for d in range(CLASSES)
            ]
            chosen = jnp.where(in_first, rows[0], jnp.where(in_second, rows[1], rows[2]))
            total[i % 4] += chosen * product[OWN * i : OWN * (i + 1), :]
        total = (total[0] + total[1]) + (total[2] + total[3])
        terms_out[2 * chip] = total[:, :128]
        terms_out[2 * chip + 1] = total[:, 128:]
        give(2 * chip + 1 - c).start()

        @pl.when(k == 0)
        def _():
            terms[me] = terms_out[me]

        @pl.when(k > 0)
        def _():
            give(2 * chip + c).start()

        return carry

    lax.fori_loop(0, 4, step, 0)

    others = [(me + v) % 8 for v in range(1, 8)]
    for other in others:
        take(other).wait_recv()
    scaled = collision_update * terms[...].reshape(64, 128)
    high = scaled.astype(jnp.bfloat16)
    low = (scaled - high.astype(jnp.float32)).astype(jnp.bfloat16)
    updated[...] = (
        base[pl.ds(0, ROWS), :]
        + jnp.dot(placing[...], high, preferred_element_type=jnp.float32)
        + jnp.dot(placing[...], low, preferred_element_type=jnp.float32)
    )
    for copy in own + edges:
        copy.wait_send()
    for side in range(2):
        over_z(me, side, 4 + side, right).wait_send()
        for i in (2, 4, 6):
            over_chip(me, side, i + side).wait_send()
    for other in others:
        give(other).wait_send()


def finish(updated, terms, updated_hbm, collision_hbm, sems):
    copies = [pltpu.make_async_copy(updated, updated_hbm, sems.at[8])]
    for slot in range(8):
        copies.append(
            pltpu.make_async_copy(
                terms.at[slot], collision_hbm.at[:, pl.ds(128 * slot, 128)], sems.at[slot]
            )
        )
    for copy in copies:
        copy.start()
    for copy in copies:
        copy.wait()


def shards(spaces, state, tensor, table, thermal, output_mode_row):
    f32, bf16 = jnp.float32, jnp.bfloat16
    flat = jnp.transpose(tensor, (1, 0, 2)).reshape(MODES * OWN, ROWS)
    anywhere = pl.BlockSpec(memory_space=pl.ANY)
    updated, terms = pl.pallas_call(
        functools.partial(kernel, spaces),
        out_shape=(pltpu.VMEM((ROWS, 128), f32), pltpu.VMEM((8, OWN, 128), f32)),
        in_specs=[anywhere] * 5,
        scratch_shapes=[
            pltpu.VMEM((896, 128), f32),
            pltpu.VMEM((MODES * OWN, ROWS), bf16),
            pltpu.VMEM((3, MODES), jnp.int32),
            pltpu.VMEM((1, CLASSES), f32),
            pltpu.VMEM((1, 64), jnp.int32),
            pltpu.VMEM((8, PAD, 128), bf16),
            pltpu.VMEM((ROWS, 256), f32),
            pltpu.VMEM((8, OWN, 128), f32),
            pltpu.VMEM((2, 8, 128), f32),
            pltpu.VMEM((2, 8, 128), f32),
            pltpu.VMEM((MODES, MODES), f32),
            pltpu.VMEM((896, 128), f32),
            pltpu.VMEM((896, 128), f32),
            pltpu.VMEM((ROWS, 64), bf16),
            pltpu.SemaphoreType.DMA((5,)),
            pltpu.SemaphoreType.DMA((6,)),
            pltpu.SemaphoreType.DMA((6,)),
            pltpu.SemaphoreType.DMA((8,)),
            pltpu.SemaphoreType.DMA((8,)),
            pltpu.SemaphoreType.DMA((8,)),
            pltpu.SemaphoreType.DMA((8,)),
            pltpu.SemaphoreType.DMA((2,)),
            pltpu.SemaphoreType.DMA((2,)),
        ],
        compiler_params=pltpu.CompilerParams(collective_id=0, has_side_effects=True),
    )(state, flat, table.T, thermal.reshape(1, CLASSES), output_mode_row.reshape(1, 64))
    return pl.pallas_call(
        finish,
        out_shape=(
            jax.ShapeDtypeStruct((ROWS, 128), f32),
            jax.ShapeDtypeStruct((OWN, 1024), f32),
        ),
        in_specs=[pl.BlockSpec(memory_space=pltpu.VMEM)] * 2,
        out_specs=(anywhere,) * 2,
        scratch_shapes=[pltpu.SemaphoreType.DMA((9,))],
    )(pltpu.with_memory_space_constraint(updated, pltpu.VMEM), pltpu.with_memory_space_constraint(terms, pltpu.VMEM))


def solution(mesh):
    in_specs = (P(None, ("space", "mode")), P("mode", None, None), P(), P(), P())
    out_specs = (P(None, ("space", "mode")), P("mode", "space"))
    return jax.shard_map(
        functools.partial(shards, mesh.shape["space"]),
        mesh=mesh,
        in_specs=in_specs,
        out_specs=out_specs,
        check_vma=False,
    )
```

time: 48.9 us -> 36.5 us (0.75)
  the two profiles are of different devices: /device:TPU:125 before, /device:TPU:1 now
where the time goes in v2:
time: 36.5 us; the launch traced here: 36.3 us
  Pallas kernels  35.7 us (98%)
  between operations  0.64 us (2%)
    pallas_call x1, Pallas kernels, shards(): pl.pallas_call(functools.partial(kernel, spaces), out_shape=(pltpu.VMEM((...  34.8 us
    pallas_call x1, Pallas kernels, shards(): pl.pallas_call(finish, out_shape=(jax.ShapeDtypeStruct((ROWS, 128), f32),...  0.86 us

profile of v2, /device:TPU:1, one launch (start us, length us, event | category | flops | bytes accessed | tf_op | source)
XLA Modules:
  0.0 36.3 jit_solution(15241888661705018463)
XLA Ops:
  0.6 34.8 %shard_map.68 = (f32[858,128]{1,0:T(8,128)S(1)}, f32[8,8,128]{2,1,0:T(8,128)S(1)}) custom-call(f32[858,128]{1,0:T(8,128)} %state_hbm.1, bf16[2288,858]{1,0:T(8,128)(2,1)} %bitcast.6, s32[3,286]{1,0:T(4,128)} %bitcast.7, f32[1,3]{1,0:T(1,128)} %bitcast.8, s32[1,64]{1,0:T(1,128)} %bitcast.9), custom_call_target="tpu_custom_call" | custom-call | tf_op jit(solution)/shard_map/pallas_call | solution.py:325
  35.5 0.9 %shard_map.69 = (f32[858,128]{1,0:T(8,128)}, f32[8,1024]{1,0:T(8,128)}) custom-call(f32[858,128]{1,0:T(8,128)S(1)} %get-tuple-element.4.updated, f32[8,8,128]{2,1,0:T(8,128)S(1)} %get-tuple-element.5.terms), custom_call_target="tpu_custom_call" | custom-call | tf_op jit(solution)/shard_map/pallas_call | solution.py:356

commit v3 on v2

--- a/solution.py
+++ b/solution.py
@@ -148,8 +148,9 @@
     matrix[...] = jnp.where(gap == 144.0, jnp.sqrt(n + 1.0), 0.0) + jnp.where(
         gap == -144.0, jnp.sqrt(n), 0.0
     )
-    row_index = lax.broadcasted_iota(jnp.int32, (ROWS, 64), 0)
-    placing[...] = jnp.where(row_index == target[...], 1.0, 0.0).astype(jnp.bfloat16)
+    row_index = lax.broadcasted_iota(jnp.int32, (ROWS, 128), 0)
+    twice = jnp.concatenate([target[...], target[...]], axis=1)
+    placing[...] = jnp.where(row_index == twice, 1.0, 0.0).astype(jnp.bfloat16)
 
     spot = lax.broadcasted_iota(jnp.int32, (OWN, 64), 1) - lax.broadcasted_iota(
         jnp.int32, (OWN, 64), 0
@@ -208,6 +209,14 @@
     def side_chip(side):
         return jnp.where(side == 0, left_q, right_q)
 
+    near_q, next_q = side_chip(near), side_chip(1 - near)
+    order = (
+        q,
+        jnp.where(q == 2, far_q, near_q),
+        jnp.where(q == 2, near_q, jnp.where(q == 3, far_q, next_q)),
+        jnp.where(q < 2, far_q, next_q),
+    )
+
     def pass_early(side):
         slot, back = 2 * side_chip(side) + c, 2 * side_chip(1 - side) + c
         over_z(slot, side, side, back).wait_recv()
@@ -219,42 +228,42 @@
         over_z(slot, 1 - side, 2 + side, back).wait_recv()
         over_chip(slot, 1 - side, 4 + side).start()
 
-    def await_partner(side):
-        slot = 2 * side_chip(side) + 1 - c
-        over_chip(slot, side, 2 + side).wait_recv()
-        over_chip(slot, 1 - side, 4 + side).wait_recv()
+    def pass_far():
+        for side in range(2):
+            over_z(far, side, 4 + side, right).wait_recv()
+            over_chip(far, side, 6 + side).start()
+
+    def await_partner(chip):
+        slot = 2 * chip + 1 - c
+        low = jnp.where(chip == left_q, 2, jnp.where(chip == right_q, 5, 6))
+        high = jnp.where(chip == left_q, 4, jnp.where(chip == right_q, 3, 7))
+        over_chip(slot, 0, low).wait_recv()
+        over_chip(slot, 1, high).wait_recv()
 
     def step(k, carry):
+        chip = jnp.where(k == 0, order[0], jnp.where(k == 1, order[1], jnp.where(k == 2, order[2], order[3])))
+
         @pl.when(k == 0)
         def _():
+            pass_early(0)
+            pass_early(1)
             tensor_load.wait()
             over_chip(partner, 0, 0).wait_recv()
             over_chip(partner, 1, 1).wait_recv()
 
         @pl.when(k == 1)
         def _():
-            pass_early(0)
-            pass_early(1)
-            transport()
             pass_late(sides[0])
             pass_late(sides[1])
-            await_partner(sides[0])
-
-        @pl.when(k == 2)
-        def _():
-            await_partner(sides[1])
-
-        @pl.when(k == 3)
-        def _():
-            for side in range(2):
-                over_z(far, side, 4 + side, right).wait_recv()
-                over_chip(far, side, 6 + side).start()
-            for side in range(2):
-                over_chip(2 * far_q + 1 - c, side, 6 + side).wait_recv()
-
-        chip = jnp.where(
-            k == 0, q, jnp.where(k == 1, side_chip(near), jnp.where(k == 2, side_chip(1 - near), far_q))
-        )
+
+        @pl.when(k == jnp.where(q == 2, 1, 2))
+        def _():
+            pass_far()
+
+        @pl.when(k > 0)
+        def _():
+            await_partner(chip)
+
         rhs = jnp.concatenate([slab[2 * chip], slab[2 * chip + 1]], axis=1)[:ROWS, :]
         first[...] = rhs.astype(jnp.float32)
         product = jnp.dot(tensor[...], rhs, preferred_element_type=jnp.float32)
@@ -283,6 +292,8 @@
 
     lax.fori_loop(0, 4, step, 0)
 
+    transport()
+
     others = [(me + v) % 8 for v in range(1, 8)]
     for other in others:
         take(other).wait_recv()
@@ -291,8 +302,11 @@
     low = (scaled - high.astype(jnp.float32)).astype(jnp.bfloat16)
     updated[...] = (
         base[pl.ds(0, ROWS), :]
-        + jnp.dot(placing[...], high, preferred_element_type=jnp.float32)
-        + jnp.dot(placing[...], low, preferred_element_type=jnp.float32)
+        + jnp.dot(
+            placing[...],
+            jnp.concatenate([high, low], axis=0),
+            preferred_element_type=jnp.float32,
+        )
     )
     for copy in own + edges:
         copy.wait_send()
@@ -305,7 +319,12 @@
 
 
 def finish(updated, terms, updated_hbm, collision_hbm, sems):
-    copies = [pltpu.make_async_copy(updated, updated_hbm, sems.at[8])]
+    copies = []
+    for part in range(4):
+        rows = pl.ds(216 * part, min(216, ROWS - 216 * part))
+        copies.append(
+            pltpu.make_async_copy(updated.at[rows], updated_hbm.at[rows], sems.at[8 + part])
+        )
     for slot in range(8):
         copies.append(
             pltpu.make_async_copy(
@@ -340,7 +359,7 @@
             pltpu.VMEM((MODES, MODES), f32),
             pltpu.VMEM((896, 128), f32),
             pltpu.VMEM((896, 128), f32),
-            pltpu.VMEM((ROWS, 64), bf16),
+            pltpu.VMEM((ROWS, 128), bf16),
             pltpu.SemaphoreType.DMA((5,)),
             pltpu.SemaphoreType.DMA((6,)),
             pltpu.SemaphoreType.DMA((6,)),
@@ -361,7 +380,7 @@
         ),
         in_specs=[pl.BlockSpec(memory_space=pltpu.VMEM)] * 2,
         out_specs=(anywhere,) * 2,
-        scratch_shapes=[pltpu.SemaphoreType.DMA((9,))],
+        scratch_shapes=[pltpu.SemaphoreType.DMA((12,))],
     )(pltpu.with_memory_space_constraint(updated, pltpu.VMEM), pltpu.with_memory_space_constraint(terms, pltpu.VMEM))
 
 

time: 36.5 us -> 35.8 us (0.981)
  Pallas kernels: 35.7 us -> 34.7 us
    pallas_call x1, Pallas kernels: 34.8 us -> 33.8 us  [shards(): pl.pallas_call(functools.partial(kernel, spaces), out_shape=(pltpu.VMEM((...]
where the time goes in v3:
time: 35.8 us; the launch traced here: 35.4 us
  Pallas kernels  34.7 us (97%)
  between operations  0.64 us (2%)
    pallas_call x1, Pallas kernels, shards(): pl.pallas_call(functools.partial(kernel, spaces), out_shape=(pltpu.VMEM((...  33.8 us
    pallas_call x1, Pallas kernels, shards(): pl.pallas_call(finish, out_shape=(jax.ShapeDtypeStruct((ROWS, 128), f32),...  0.88 us

profile of v3, /device:TPU:1, one launch (start us, length us, event | category | flops | bytes accessed | tf_op | source)
XLA Modules:
  0.0 35.4 jit_solution(8215440775397101660)
XLA Ops:
  0.6 33.8 %shard_map.68 = (f32[858,128]{1,0:T(8,128)S(1)}, f32[8,8,128]{2,1,0:T(8,128)S(1)}) custom-call(f32[858,128]{1,0:T(8,128)} %state_hbm.1, bf16[2288,858]{1,0:T(8,128)(2,1)} %bitcast.6, s32[3,286]{1,0:T(4,128)} %bitcast.7, f32[1,3]{1,0:T(1,128)} %bitcast.8, s32[1,64]{1,0:T(1,128)} %bitcast.9), custom_call_target="tpu_custom_call" | custom-call | tf_op jit(solution)/shard_map/pallas_call | solution.py:344
  34.5 0.9 %shard_map.69 = (f32[858,128]{1,0:T(8,128)}, f32[8,1024]{1,0:T(8,128)}) custom-call(f32[858,128]{1,0:T(8,128)S(1)} %get-tuple-element.4.updated, f32[8,8,128]{2,1,0:T(8,128)S(1)} %get-tuple-element.5.terms), custom_call_target="tpu_custom_call" | custom-call | tf_op jit(solution)/shard_map/pallas_call | solution.py:375

commit v4 on v3

--- a/solution.py
+++ b/solution.py
@@ -82,7 +82,10 @@
         copy.start()
         return copy
 
-    state_load = load(state_hbm, state.at[pl.ds(0, ROWS)], 0)
+    state_loads = []
+    for part in range(4):
+        rows = pl.ds(216 * part, min(216, ROWS - 216 * part))
+        state_loads.append(load(state_hbm.at[rows], state.at[rows], 5 + part))
     table_load = load(table_hbm, table, 2)
     thermal_load = load(thermal_hbm, thermal, 3)
     target_load = load(target_hbm, target, 4)
@@ -106,10 +109,24 @@
     def over_chip(slot, h, i):
         return remote(half(slot, h), half(slot, h), c_send.at[i], c_recv.at[i], {"mode": partner})
 
-    state_load.wait()
+    for copy in state_loads:
+        copy.wait()
     tensor_load = load(tensor_hbm, tensor, 1)
     state[pl.ds(ROWS, 896 - ROWS), :] = jnp.zeros((896 - ROWS, 128), jnp.float32)
     slab[me] = state[pl.ds(0, PAD), :].astype(jnp.bfloat16)
+
+    pl.semaphore_wait(barrier, 4)
+
+    own = [
+        over_z(me, 0, 0, right),
+        over_z(me, 1, 1, left),
+        over_z(me, 1, 2, right),
+        over_z(me, 0, 3, left),
+        over_chip(me, 0, 0),
+        over_chip(me, 1, 1),
+    ]
+    for copy in own:
+        copy.start()
 
     edge_out[...] = jnp.zeros_like(edge_out)
     for t in range(7):
@@ -120,17 +137,7 @@
         remote(edge_out.at[0], edge_in.at[1], e_send.at[0], e_recv.at[0], before_id),
         remote(edge_out.at[1], edge_in.at[0], e_send.at[1], e_recv.at[1], after_id),
     ]
-    pl.semaphore_wait(barrier, 4)
-
-    own = [
-        over_z(me, 0, 0, right),
-        over_z(me, 1, 1, left),
-        over_z(me, 1, 2, right),
-        over_z(me, 0, 3, left),
-        over_chip(me, 0, 0),
-        over_chip(me, 1, 1),
-    ]
-    for copy in edges + own:
+    for copy in edges:
         copy.start()
 
     table_load.wait()
@@ -360,7 +367,7 @@
             pltpu.VMEM((896, 128), f32),
             pltpu.VMEM((896, 128), f32),
             pltpu.VMEM((ROWS, 128), bf16),
-            pltpu.SemaphoreType.DMA((5,)),
+            pltpu.SemaphoreType.DMA((9,)),
             pltpu.SemaphoreType.DMA((6,)),
             pltpu.SemaphoreType.DMA((6,)),
             pltpu.SemaphoreType.DMA((8,)),

time: 35.8 us -> 35.5 us (level)
  no operation moved by 1% of the time
where the time goes in v4:
time: 35.5 us; the launch traced here: 35.4 us
  Pallas kernels  34.8 us (98%)
  between operations  0.64 us (2%)
    pallas_call x1, Pallas kernels, shards(): pl.pallas_call(functools.partial(kernel, spaces), out_shape=(pltpu.VMEM((...  33.9 us
    pallas_call x1, Pallas kernels, shards(): pl.pallas_call(finish, out_shape=(jax.ShapeDtypeStruct((ROWS, 128), f32),...  0.88 us

profile of v4, /device:TPU:1, one launch (start us, length us, event | category | flops | bytes accessed | tf_op | source)
XLA Modules:
  0.0 35.4 jit_solution(12816972032423124624)
XLA Ops:
  0.6 33.9 %shard_map.68 = (f32[858,128]{1,0:T(8,128)S(1)}, f32[8,8,128]{2,1,0:T(8,128)S(1)}) custom-call(f32[858,128]{1,0:T(8,128)} %state_hbm.1, bf16[2288,858]{1,0:T(8,128)(2,1)} %bitcast.6, s32[3,286]{1,0:T(4,128)} %bitcast.7, f32[1,3]{1,0:T(1,128)} %bitcast.8, s32[1,64]{1,0:T(1,128)} %bitcast.9), custom_call_target="tpu_custom_call" | custom-call | tf_op jit(solution)/shard_map/pallas_call | solution.py:351
  34.5 0.9 %shard_map.69 = (f32[858,128]{1,0:T(8,128)}, f32[8,1024]{1,0:T(8,128)}) custom-call(f32[858,128]{1,0:T(8,128)S(1)} %get-tuple-element.4.updated, f32[8,8,128]{2,1,0:T(8,128)S(1)} %get-tuple-element.5.terms), custom_call_target="tpu_custom_call" | custom-call | tf_op jit(solution)/shard_map/pallas_call | solution.py:382

commit v5 on v4

--- a/solution.py
+++ b/solution.py
@@ -125,7 +125,7 @@
         over_chip(me, 0, 0),
         over_chip(me, 1, 1),
     ]
-    for copy in own:
+    for copy in own[4:] + own[:4]:
         copy.start()
 
     edge_out[...] = jnp.zeros_like(edge_out)

time: 35.5 us -> 35.5 us (level)
  no operation moved by 1% of the time
where the time goes in v5:
time: 35.5 us; the launch traced here: 35.4 us
  Pallas kernels  34.8 us (98%)
  between operations  0.64 us (2%)
    pallas_call x1, Pallas kernels, shards(): pl.pallas_call(functools.partial(kernel, spaces), out_shape=(pltpu.VMEM((...  33.9 us
    pallas_call x1, Pallas kernels, shards(): pl.pallas_call(finish, out_shape=(jax.ShapeDtypeStruct((ROWS, 128), f32),...  0.88 us

profile of v5, /device:TPU:1, one launch (start us, length us, event | category | flops | bytes accessed | tf_op | source)
XLA Modules:
  0.0 35.4 jit_solution(1075846628154447010)
XLA Ops:
  0.6 33.9 %shard_map.68 = (f32[858,128]{1,0:T(8,128)S(1)}, f32[8,8,128]{2,1,0:T(8,128)S(1)}) custom-call(f32[858,128]{1,0:T(8,128)} %state_hbm.1, bf16[2288,858]{1,0:T(8,128)(2,1)} %bitcast.6, s32[3,286]{1,0:T(4,128)} %bitcast.7, f32[1,3]{1,0:T(1,128)} %bitcast.8, s32[1,64]{1,0:T(1,128)} %bitcast.9), custom_call_target="tpu_custom_call" | custom-call | tf_op jit(solution)/shard_map/pallas_call | solution.py:351
  34.5 0.9 %shard_map.69 = (f32[858,128]{1,0:T(8,128)}, f32[8,1024]{1,0:T(8,128)}) custom-call(f32[858,128]{1,0:T(8,128)S(1)} %get-tuple-element.4.updated, f32[8,8,128]{2,1,0:T(8,128)S(1)} %get-tuple-element.5.terms), custom_call_target="tpu_custom_call" | custom-call | tf_op jit(solution)/shard_map/pallas_call | solution.py:382
